TPU v7x, 32 devices: a whole 2x2x4 slice. The times are simulated.
32 devices in a mesh: grp: 2 (over y), dp: 4 (over x, core), slab: 4 (over z).
Axes of the slice: x: 2, y: 2, z: 4, core: 2. Of those that a mesh axis runs over, the one named last changes fastest.
Arguments:
- feats: bfloat16 [8, 32, 32, 128, 128], P(('grp', 'dp'), None, 'slab'), parts along dimension 0, may hold values from -6 to 6
- grains: int32 [8, 32, 128, 128], P(('grp', 'dp'), 'slab'), parts along dimension 0, may hold values from 0 to 4095
- spec_weight: bfloat16 [256, 16, 2048], P('slab'), may hold values from -0.75 to 0.75
- taps: float32 [27, 32], replicated, may hold values from -1.25 to 1.25
- point_weight: bfloat16 [32, 32], replicated, may hold values from -1 to 1
- bias: float32 [32], replicated, may hold values from -4 to 4
- cotangent: bfloat16 [8, 32, 32, 128, 128], P(('grp', 'dp'), None, 'slab'), parts along dimension 0, may hold values from -3 to 3
Outputs:
- grad_feats: bfloat16 [8, 32, 32, 128, 128], P(('grp', 'dp'), None, 'slab'), parts along dimension 0
- grad_spec: float32 [256, 32, 2048], P('slab', 'grp', 'dp'), parts along dimension 1
There are 2 independent parts, one for each index of `grp`. A program takes and returns all parts, laid end to end along the dimension named above; an argument that names none is the same for every part. Nothing has to cross between parts.
All inputs are finite; a program needn't handle non-finite values.
Results may differ from a plain program's by a relative error of at most 0.017.
Values may be sent and summed in bfloat16 or wider, within the bound.
A program may use at most 192 MiB of HBM per device.

v0:
```python
import math
import jax
import jax.numpy as jnp
from jax import lax
from jax.sharding import PartitionSpec as P

NX = 128
NY = 128
NZ = 32
KX = 16
KY = 16
KZ = 16
HIGHEST = lax.Precision.HIGHEST


def extended(shard, sides, width):
    for axis, dim in sides:
        size, length = (lax.axis_size(axis), shard.shape[dim])
        up = [(i, (i + 1) % size) for i in range(size - 1)]
        down = [(j, i) for i, j in up]
        last = lax.slice_in_dim(shard, length - width, length, axis=dim)
        first = lax.slice_in_dim(shard, 0, width, axis=dim)
        before = lax.ppermute(last, axis, up)
        after = lax.ppermute(first, axis, down)
        shard = jnp.concatenate([before, shard, after], axis=dim)
    return shard


def tables(count, length, span):
    indices = jnp.arange(count, dtype=jnp.int32)
    frequency = jnp.where(indices < count // 2, indices, length - count + indices)
    position = jnp.arange(span, dtype=jnp.int32)
    phases = frequency[:, None] * position[None, :] % length
    angles = phases.astype(jnp.float32) * (2.0 * math.pi / length)
    return (jnp.cos(angles), jnp.sin(angles))


def mobility(grains):
    leading = [(0, 0)] * (grains.ndim - 2)
    along_x = (grains[..., 1:, :] != grains[..., :-1, :]).astype(jnp.float32)
    along_y = (grains[..., :, 1:] != grains[..., :, :-1]).astype(jnp.float32)
    differ = jnp.pad(along_x, leading + [(1, 0), (0, 0)]) + jnp.pad(
        along_x, leading + [(0, 1), (0, 0)]
    )
    differ = (
        differ
        + jnp.pad(along_y, leading + [(0, 0), (1, 0)])
        + jnp.pad(along_y, leading + [(0, 0), (0, 1)])
    )
    return 0.25 * (1.0 + differ)


def stencil(padded, taps, adjoint):
    planes = padded.shape[-3] - 2
    rows_x = padded.shape[-2] - 2
    rows_y = padded.shape[-1] - 2
    total = jnp.zeros(padded.shape[:-3] + (planes, rows_x, rows_y), jnp.float32)
    for offset in range(27):
        shift_z, shift_x, shift_y = (offset // 9, offset // 3 % 3, offset % 3)
        if adjoint:
            shift_z, shift_x, shift_y = (2 - shift_z, 2 - shift_x, 2 - shift_y)
        window = padded[
            ..., shift_z : shift_z + planes, shift_x : shift_x + rows_x, shift_y : shift_y + rows_y
        ]
        total = total + taps[offset][:, None, None, None] * window.astype(jnp.float32)
    return total


def plane_forward(field, cos_x, sin_x, cos_y, sin_y):
    real_y = jnp.einsum("...xy,ky->...xk", field, cos_y, precision=HIGHEST)
    imag_y = -jnp.einsum("...xy,ky->...xk", field, sin_y, precision=HIGHEST)
    real_part = jnp.einsum("...xk,jx->...jk", real_y, cos_x, precision=HIGHEST) + jnp.einsum(
        "...xk,jx->...jk", imag_y, sin_x, precision=HIGHEST
    )
    imag_part = jnp.einsum("...xk,jx->...jk", imag_y, cos_x, precision=HIGHEST) - jnp.einsum(
        "...xk,jx->...jk", real_y, sin_x, precision=HIGHEST
    )
    return (real_part, imag_part)


def plane_inverse(real_part, imag_part, cos_x, sin_x, cos_y, sin_y):
    real_x = jnp.einsum("...jk,jx->...xk", real_part, cos_x, precision=HIGHEST) - jnp.einsum(
        "...jk,jx->...xk", imag_part, sin_x, precision=HIGHEST
    )
    imag_x = jnp.einsum("...jk,jx->...xk", imag_part, cos_x, precision=HIGHEST) + jnp.einsum(
        "...jk,jx->...xk", real_part, sin_x, precision=HIGHEST
    )
    return jnp.einsum("...xk,ky->...xy", real_x, cos_y, precision=HIGHEST) - jnp.einsum(
        "...xk,ky->...xy", imag_x, sin_y, precision=HIGHEST
    )


def depth_forward(packed, cos_table, sin_table):
    width = packed.shape[-1] // 2
    real_in = packed[..., :width]
    imag_in = packed[..., width:]
    real_out = jnp.einsum("pszc,kz->pskc", real_in, cos_table, precision=HIGHEST) + jnp.einsum(
        "pszc,kz->pskc", imag_in, sin_table, precision=HIGHEST
    )
    imag_out = jnp.einsum("pszc,kz->pskc", imag_in, cos_table, precision=HIGHEST) - jnp.einsum(
        "pszc,kz->pskc", real_in, sin_table, precision=HIGHEST
    )
    return jnp.concatenate([real_out, imag_out], axis=-1)


def depth_inverse(real_modes, imag_modes, cos_table, sin_table):
    real_out = jnp.einsum("pskc,kz->pszc", real_modes, cos_table, precision=HIGHEST) - jnp.einsum(
        "pskc,kz->pszc", imag_modes, sin_table, precision=HIGHEST
    )
    imag_out = jnp.einsum("pskc,kz->pszc", imag_modes, cos_table, precision=HIGHEST) + jnp.einsum(
        "pskc,kz->pszc", real_modes, sin_table, precision=HIGHEST
    )
    return jnp.concatenate([real_out, imag_out], axis=-1)


def rim_planes(field):
    return extended(field, (("slab", 2),), 1)


def local(feats, grains, spec_weight, taps, point_weight, bias, cotangent):
    samples_here = feats.shape[0]
    channels = feats.shape[1]
    planes = feats.shape[2]
    cos_x, sin_x = tables(KX, NX, NX)
    cos_y, sin_y = tables(KY, NY, NY)
    cos_full, sin_full = tables(KZ, NZ, NZ)
    cell_scale = math.sqrt(NX * NY * NZ)
    mode_scale = math.sqrt(KX * KY * KZ)
    mode_rows = spec_weight.shape[0]
    weights = spec_weight.astype(jnp.float32).reshape(mode_rows, KZ, 2, channels, channels)
    w_real = weights[:, :, 0]
    w_imag = weights[:, :, 1]
    moving = mobility(grains)[:, None]

    def to_modes(field):
        real_plane, imag_plane = plane_forward(field, cos_x, sin_x, cos_y, sin_y)
        packed = jnp.stack([real_plane, imag_plane], axis=1)
        packed = packed.transpose(4, 5, 0, 3, 1, 2).reshape(
            KX * KY, samples_here, planes, 2 * channels
        )
        moved = lax.all_to_all(packed, "slab", split_axis=0, concat_axis=2, tiled=True)
        summed = depth_forward(moved, cos_full, sin_full)
        return (summed[..., :channels], summed[..., channels:])

    def from_modes(real_modes, imag_modes):
        planar = depth_inverse(real_modes, imag_modes, cos_full, sin_full)
        packed = lax.all_to_all(planar, "slab", split_axis=2, concat_axis=0, tiled=True)
        grouped = packed.reshape(KX, KY, samples_here, planes, 2, channels).transpose(
            2, 4, 5, 3, 0, 1
        )
        return plane_inverse(grouped[:, 0], grouped[:, 1], cos_x, sin_x, cos_y, sin_y)

    zero_rim = ((0, 0), (0, 0), (0, 0), (1, 1), (1, 1))
    padded = jnp.pad(rim_planes(feats), zero_rim)
    smooth = stencil(padded, taps, False).astype(jnp.bfloat16)
    local_part = moving * jnp.einsum(
        "sczxy,co->sozxy", smooth, point_weight, preferred_element_type=jnp.float32
    )
    spec_real, spec_imag = to_modes(feats.astype(jnp.float32))
    spec_real = spec_real / cell_scale
    spec_imag = spec_imag / cell_scale
    mixed_real = jnp.einsum("pskc,pkco->psko", spec_real, w_real, precision=HIGHEST) - jnp.einsum(
        "pskc,pkco->psko", spec_imag, w_imag, precision=HIGHEST
    )
    mixed_imag = jnp.einsum("pskc,pkco->psko", spec_real, w_imag, precision=HIGHEST) + jnp.einsum(
        "pskc,pkco->psko", spec_imag, w_real, precision=HIGHEST
    )
    spectral = from_modes(mixed_real, mixed_imag) / mode_scale
    pre = spectral + local_part + bias[None, :, None, None, None]
    gate = jax.nn.sigmoid(pre)
    delta = (cotangent.astype(jnp.float32) * gate * (1.0 + pre * (1.0 - gate))).astype(jnp.bfloat16)
    dual_real, dual_imag = to_modes(delta.astype(jnp.float32))
    dual_real = dual_real / mode_scale
    dual_imag = dual_imag / mode_scale
    batch_total = samples_here * lax.axis_size("dp")
    grad_real = jnp.einsum("pskc,psko->pkco", spec_real, dual_real, precision=HIGHEST) + jnp.einsum(
        "pskc,psko->pkco", spec_imag, dual_imag, precision=HIGHEST
    )
    grad_imag = jnp.einsum("pskc,psko->pkco", spec_real, dual_imag, precision=HIGHEST) - jnp.einsum(
        "pskc,psko->pkco", spec_imag, dual_real, precision=HIGHEST
    )
    grad_terms = (jnp.stack([grad_real, grad_imag], axis=2) / batch_total).reshape(
        mode_rows, KZ, 2 * channels * channels
    )
    grad_spec = lax.psum_scatter(
        grad_terms.astype(jnp.bfloat16), "dp", scatter_dimension=2, tiled=True
    ).astype(jnp.float32)
    back_real = jnp.einsum("psko,pkco->pskc", dual_real, w_real, precision=HIGHEST) + jnp.einsum(
        "psko,pkco->pskc", dual_imag, w_imag, precision=HIGHEST
    )
    back_imag = jnp.einsum("psko,pkco->pskc", dual_imag, w_real, precision=HIGHEST) - jnp.einsum(
        "psko,pkco->pskc", dual_real, w_imag, precision=HIGHEST
    )
    spectral_back = from_modes(back_real, back_imag) / cell_scale
    spread = (
        moving
        * jnp.einsum("sozxy,co->sczxy", delta, point_weight, preferred_element_type=jnp.float32)
    ).astype(jnp.bfloat16)
    spread_padded = jnp.pad(rim_planes(spread), zero_rim)
    local_back = stencil(spread_padded, taps, True)
    grad_feats = (spectral_back + local_back).astype(jnp.bfloat16)
    return (grad_feats, grad_spec)


def solution(mesh):
    in_specs = (
        P(("grp", "dp"), None, "slab", None, None),
        P(("grp", "dp"), "slab", None, None),
        P("slab", None, None),
        P(),
        P(),
        P(),
        P(("grp", "dp"), None, "slab", None, None),
    )
    out_specs = (P(("grp", "dp"), None, "slab", None, None), P("slab", "grp", "dp"))
    return jax.shard_map(local, mesh=mesh, in_specs=in_specs, out_specs=out_specs, check_vma=False)
```

profile of v0, /device:TPU:0, one launch (start us, length us, event | category | flops | bytes accessed | tf_op | source)
XLA Modules:
  0.0 829.7 jit_solution(2616619679292924234)
XLA Ops:
  7.2 3.3 fusion.382
  10.5 1.4 collective-permute-start.1
  11.9 6.6 collective-permute-start
  18.5 9.4 %negate_bitcast_fusion = f32[32,8,128,16]{2,3,1,0:T(8,128)S(1)} fusion(bf16[1,32,8,128,128]{4,3,2,1,0:T(8,128)(2,1)} %param.7, s32[16]{0:T(128)S(1)} %compare_select_fusion.1), kind=kOutput, calls=%fused_computation.86 | convolution fusion | flops 805859328 | bytes 10485824 | tf_op jit(solution)/shard_map/...xy,ky->...xk/dot_general | solution.py:71
  27.9 6.8 fusion.67
  34.6 8.4 %fusion.58 = f32[16,32,8,16]{1,0,3,2:T(8,128)S(1)} fusion(f32[32,8,128,16]{2,3,1,0:T(8,128)S(1)} %negate_bitcast_fusion, s32[16]{0:T(128)S(1)} %compare_select_fusion.1), kind=kOutput, calls=%fused_computation.95 | convolution fusion | flops 100691968 | bytes 2359360 | tf_op jit(solution)/shard_map/...xk,jx->...jk/dot_general | solution.py:75
  43.0 8.6 %fusion.60 = f32[16,32,8,16]{1,0,3,2:T(8,128)S(1)} fusion(f32[32,8,128,16]{2,3,1,0:T(8,128)S(1)} %negate_bitcast_fusion, s32[16]{0:T(128)S(1)} %compare_select_fusion.1), kind=kOutput, calls=%fused_computation.97 | convolution fusion | flops 100691968 | bytes 2359360 | tf_op jit(solution)/shard_map/...xk,jx->...jk/dot_general | solution.py:72
  51.6 8.4 %fusion.81 = f32[1,1,32,8,16,16]{2,4,5,3,1,0:T(8,128)S(1)} fusion(f32[16,32,8,16]{1,0,3,2:T(8,128)S(1)} %fusion.58, f32[32,8,128,16]{2,3,1,0:T(8,128)S(1)} %fusion.67, s32[16]{0:T(128)S(1)} %compare_select_fusion.1), kind=kOutput, calls=%fused_computation.109 | convolution fusion | flops 100757504 | bytes 2621504 | tf_op jit(solution)/shard_map/...xk,jx->...jk/dot_general | solution.py:75
  59.9 8.4 %fusion.75 = f32[1,1,32,8,16,16]{2,4,5,3,1,0:T(8,128)S(1)} fusion(f32[16,32,8,16]{1,0,3,2:T(8,128)S(1)} %fusion.60, f32[32,8,128,16]{2,3,1,0:T(8,128)S(1)} %fusion.67, s32[16]{0:T(128)S(1)} %compare_select_fusion.1), kind=kOutput, calls=%fused_computation.107 | convolution fusion | flops 100757504 | bytes 2621504 | tf_op jit(solution)/shard_map/...xk,jx->...jk/dot_general | solution.py:72
  68.5 1.6 copy.69
  70.1 2.2 reshape.358
  72.3 3.1 reshape.403
  75.4 4.3 all-to-all-start
  79.9 9.2 %copy.73 = bf16[64,16,2048]{0,2,1:T(8,128)(2,1)} copy(bf16[64,16,2048]{2,1,0:T(8,128)(2,1)} %param.9) | data formatting | bytes 8388608 | tf_op args[2]
  90.5 3.1 all-to-all-done
  94.2 2.2 reduce.16
  100.2 6.4 fusion.23
  111.2 1.5 reshape.405
  112.6 3.5 all-to-all-start.1
  116.1 23.1 %select_maximum_fusion.2 = bf16[1,32,10,130,130]{4,3,2,1,0:T(8,128)(2,1)} fusion(bf16[1,32,1,128,128]{4,3,2,1,0:T(8,128)(2,1)} %collective-permute-done.1, bf16[1,32,8,128,128]{4,3,2,1,0:T(8,128)(2,1)} %param.7, bf16[1,32,1,128,128]{4,3,2,1,0:T(8,128)(2,1)} %collective-permute-done), kind=kLoop, calls=%fused_computation.9 | loop fusion | flops 102752000 | bytes 21301760 | tf_op jit(solution)/shard_map/concatenate | solution.py:25
  139.5 183.3 %fusion.39 = bf16[32,8,128,128]{3,2,1,0:T(8,128)(2,1)} fusion(bf16[1,32,10,130,130]{4,3,2,1,0:T(8,128)(2,1)} %select_maximum_fusion.2, f32[32]{0:T(128)S(1)} %get-tuple-element.49, f32[32]{0:T(128)S(1)} %get-tuple-element.50, f32[32]{0:T(128)S(1)} %get-tuple-element.25, f32[32]{0:T(128)S(1)} %get-tuple-element.26, ...), kind=kLoop, calls=%fused_computation.69 | loop fusion | flops 348127232 | bytes 220204416 | tf_op jit(solution)/shard_map/reshape.89
  322.8 14.3 %fusion.37 = f32[8,128,128,32]{2,3,1,0:T(8,128)} fusion(bf16[32,8,128,128]{3,2,1,0:T(8,128)(2,1)} %fusion.39, bf16[32,32]{1,0:T(8,128)(2,1)S(1)} %copy-done), kind=kOutput, calls=%fused_computation.65 | convolution fusion | flops 268435456 | bytes 25167872 | tf_op jit(solution)/shard_map/sczxy,co->sozxy/dot_general | solution.py:156
  337.1 2.2 reduce.17
  340.2 1.2 reshape.364
  341.4 1.2 copy.251
  342.6 3.7 fusion.108
  346.3 3.5 fusion.109
  349.8 3.5 subtract_bitcast_fusion.2
  353.3 29.0 %fusion.48 = f32[32,8,128,128]{3,2,1,0:T(8,128)} fusion(f32[32,8,128,16]{2,0,3,1:T(8,128)S(1)} %subtract_bitcast_fusion.2, s32[16]{0:T(128)S(1)} %compare_select_fusion.1), kind=kOutput, calls=%fused_computation.79 | convolution fusion | flops 805335040 | bytes 18874432 | tf_op jit(solution)/shard_map/...xk,ky->...xy/dot_general | solution.py:88
  382.4 3.5 add_bitcast_fusion.2
  386.0 44.4 %fusion.40 = bf16[32,8,128,128]{3,2,1,0:T(8,128)(2,1)S(1)} fusion(f32[32]{0:T(128)S(1)} %copy-done.68, f32[8,128,128,32]{2,3,1,0:T(8,128)} %fusion.37, f32[8,128,128]{2,1,0:T(8,128)S(1)} %copy-done.9, f32[32,8,128,128]{3,2,1,0:T(8,128)} %fusion.48, bf16[1,32,8,128,128]{4,3,2,1,0:T(8,128)(2,1)S(1)} %bitcast.461, ...), kind=kOutput, calls=%fused_computation.70 | convolution fusion | flops 868249600 | bytes 52953280 | tf_op jit(solution)/shard_map/...xk,ky->...xy/dot_general | solution.py:88
  430.4 6.8 convolution_negate_fusion
  437.3 6.8 fusion.155
  444.1 8.4 %fusion.50 = f32[16,32,8,16]{1,0,3,2:T(8,128)S(1)} fusion(f32[32,8,128,16]{2,3,1,0:T(8,128)S(1)} %convolution_negate_fusion, s32[16]{0:T(128)S(1)} %compare_select_fusion.1), kind=kOutput, calls=%fused_computation.87 | convolution fusion | flops 100691968 | bytes 2359360 | tf_op jit(solution)/shard_map/...xk,jx->...jk/dot_general | solution.py:75
  452.4 8.6 %fusion.52 = f32[16,32,8,16]{1,0,3,2:T(8,128)S(1)} fusion(f32[32,8,128,16]{2,3,1,0:T(8,128)S(1)} %convolution_negate_fusion, s32[16]{0:T(128)S(1)} %compare_select_fusion.1), kind=kOutput, calls=%fused_computation.89 | convolution fusion | flops 100691968 | bytes 2359360 | tf_op jit(solution)/shard_map/...xk,jx->...jk/dot_general | solution.py:72
  461.0 10.8 %fusion.35 = f32[8,128,128,32]{2,3,1,0:T(8,128)} fusion(bf16[32,8,128,128]{3,2,1,0:T(8,128)(2,1)S(1)} %fusion.40, bf16[32,32]{1,0:T(8,128)(2,1)S(1)} %copy-done), kind=kOutput, calls=%fused_computation.63 | convolution fusion | flops 268435456 | bytes 25167872 | tf_op jit(solution)/shard_map/sozxy,co->sczxy/dot_general | solution.py:197
  471.8 8.7 %fusion.93 = f32[1,1,32,8,16,16]{2,4,5,3,1,0:T(8,128)S(1)} fusion(f32[16,32,8,16]{1,0,3,2:T(8,128)S(1)} %fusion.50, f32[32,8,128,16]{2,3,1,0:T(8,128)S(1)} %fusion.155, s32[16]{0:T(128)S(1)} %compare_select_fusion.1), kind=kOutput, calls=%fused_computation.113 | convolution fusion | flops 100757504 | bytes 2621504 | tf_op jit(solution)/shard_map/...xk,jx->...jk/dot_general | solution.py:75
  480.6 8.4 %fusion.87 = f32[1,1,32,8,16,16]{2,4,5,3,1,0:T(8,128)S(1)} fusion(f32[16,32,8,16]{1,0,3,2:T(8,128)S(1)} %fusion.52, f32[32,8,128,16]{2,3,1,0:T(8,128)S(1)} %fusion.155, s32[16]{0:T(128)S(1)} %compare_select_fusion.1), kind=kOutput, calls=%fused_computation.111 | convolution fusion | flops 100757504 | bytes 2621504 | tf_op jit(solution)/shard_map/...xk,jx->...jk/dot_general | solution.py:72
  489.1 1.6 copy.86
  490.7 1.1 reshape.371
  491.9 1.5 reshape.407
  493.3 5.2 all-to-all-start.2
  498.6 15.2 %fusion.66 = bf16[1,32,8,128,128]{4,3,2,1,0:T(8,128)(2,1)S(1)} fusion(f32[8,128,128,32]{2,3,1,0:T(8,128)} %fusion.35, f32[8,128,128]{2,1,0:T(8,128)} %multiply_bitcast_fusion), kind=kLoop, calls=%fused_computation.103 | loop fusion | flops 8388608 | bytes 25690112 | tf_op jit(solution)/shard_map/convert_element_type | solution.py:198
  513.8 3.3 copy-done.3
  517.1 1.4 fusion.381
  518.6 1.3 collective-permute-start.3
  519.9 5.7 collective-permute-start.2
  525.6 2.2 reduce.18
  531.5 10.0 %fusion.27 = (f32[64,16,32]{0,2,1:T(8,128)S(1)}, f32[64,16,32]{0,2,1:T(8,128)S(1)}, f32[64,16,32]{0,2,1:T(8,128)S(1)}, f32[64,16,32]{0,2,1:T(8,128)S(1)}) fusion(f32[64,16,32]{0,2,1:T(8,128)S(1)} %copy.156, bf16[64,16,2,32,32]{0,4,3,2,1:T(8,128)(2,1)} %bitcast.430, f32[64,16,32]{0,2,1:T(8,128)S(1)} %copy.157), kind=kLoop, calls=%fused_computation.51 | loop fusion | flops 10354688 | bytes 4980736
  546.1 1.5 reshape.409
  547.6 4.2 all-to-all-start.3
  551.8 2.5 add_bitcast_fusion
  554.3 4.6 fusion.4
  558.9 23.5 %select_maximum_fusion = bf16[1,32,10,130,130]{4,3,2,1,0:T(8,128)(2,1)} fusion(bf16[1,32,1,128,128]{4,3,2,1,0:T(8,128)(2,1)} %collective-permute-done.3, bf16[1,32,8,128,128]{4,3,2,1,0:T(8,128)(2,1)} %copy-done.3, bf16[1,32,1,128,128]{4,3,2,1,0:T(8,128)(2,1)} %collective-permute-done.2), kind=kLoop, calls=%fused_computation.7 | loop fusion | flops 102752000 | bytes 21301760 | tf_op jit(solution)/shard_map/concatenate | solution.py:25
  582.4 2.2 reduce.19
  585.6 1.2 reshape.376
  586.8 1.2 copy.250
  588.0 3.5 fusion.110
  591.5 3.5 fusion.111
  595.0 3.7 subtract_bitcast_fusion.1
  599.0 28.8 %fusion.45 = f32[32,8,128,128]{3,2,1,0:T(8,128)} fusion(f32[32,8,128,16]{2,0,3,1:T(8,128)S(1)} %subtract_bitcast_fusion.1, s32[16]{0:T(128)S(1)} %compare_select_fusion.1), kind=kOutput, calls=%fused_computation.75 | convolution fusion | flops 805335040 | bytes 18874432 | tf_op jit(solution)/shard_map/...xk,ky->...xy/dot_general | solution.py:88
  627.8 3.5 add_bitcast_fusion.1
  631.6 187.5 %fusion.22 = bf16[1,32,8,128,128]{4,3,2,1,0:T(8,128)(2,1)} fusion(f32[32,8,128,128]{3,2,1,0:T(8,128)} %fusion.45, bf16[1,32,10,130,130]{4,3,2,1,0:T(8,128)(2,1)} %select_maximum_fusion, bf16[1,32,8,128,128]{4,3,2,1,0:T(8,128)(2,1)} %copy-done.3, bf16[1,32,1,128,128]{4,3,2,1,0:T(8,128)(2,1)} %collective-permute-done.2, ...), kind=kOutput, calls=%fused_computation.38 | convolution fusion | flops 1174433792 | bytes 256380352 | tf_op jit(solution)/shard_map/...xk,ky->...xy/dot_general | solution.py:88
  819.1 3.5 copy.102
  (196 shorter events, 20.9 us)
Async XLA Ops:
  7.2 315.6 %copy-start = (bf16[32,32]{1,0:T(8,128)(2,1)S(1)}, bf16[32,32]{1,0:T(8,128)(2,1)}, u32[]{:S(2)}) copy-start(bf16[32,32]{1,0:T(8,128)(2,1)} %param.11) | copy-start | bytes 6148
  10.5 105.7 %collective-permute-start.1 = (bf16[1,32,1,128,128]{4,3,2,1,0:T(8,128)(2,1)}, bf16[1,32,1,128,128]{4,3,2,1,0:T(8,128)(2,1)}, u32[]{:S(2)}, u32[]{:S(2)}) collective-permute-start(bf16[1,32,1,128,128]{4,3,2,1,0:T(8,128)(2,1)} %get-tuple-element.21), channel_id=1, source_target_pairs={{1,0},{2,1},{3,2},{5,4},{6,5},{7,6},{9,8},{10,9},{11,10},{13,12},{... | collective-permute-start | bytes 3145736 | tf_op jit(solution)/shard_map/ppermute | solution.py:24
  11.9 104.3 %collective-permute-start = (bf16[1,32,1,128,128]{4,3,2,1,0:T(8,128)(2,1)}, bf16[1,32,1,128,128]{4,3,2,1,0:T(8,128)(2,1)}, u32[]{:S(2)}, u32[]{:S(2)}) collective-permute-start(bf16[1,32,1,128,128]{4,3,2,1,0:T(8,128)(2,1)} %get-tuple-element.20), channel_id=1, source_target_pairs={{0,1},{1,2},{2,3},{4,5},{5,6},{6,7},{8,9},{9,10},{10,11},{12,13},{... | collective-permute-start | bytes 3145736 | tf_op jit(solution)/shard_map/ppermute | solution.py:23
  34.6 45.1 %copy-start.4 = (s32[1,8,128,128]{3,2,1,0:T(8,128)S(1)}, s32[1,8,128,128]{3,2,1,0:T(8,128)}, u32[]{:S(2)}) copy-start(s32[1,8,128,128]{3,2,1,0:T(8,128)} %param.8) | copy-start | bytes 1572868
  75.4 18.2 %all-to-all-start = ((f32[4,1,32768]{2,1,0:T(1,128)}), f32[4,1,32768]{2,1,0:T(1,128)S(1)}, u32[]{:S(2)}, u32[]{:S(2)}) async-start(f32[4,1,32768]{2,1,0:T(1,128)} %reshape.403), calls=%async_computation | async-start | bytes 1048576 | tf_op jit(solution)/shard_map/all_to_all | solution.py:141
  90.2 49.0 %copy-start.14 = (f32[32]{0:T(128)}, f32[32]{0:T(128)S(1)}, u32[]{:S(2)}) copy-start(f32[32]{0:T(128)S(1)} %get-tuple-element.43) | copy-start | bytes 388
  90.2 49.0 %copy-start.16 = (f32[32]{0:T(128)}, f32[32]{0:T(128)S(1)}, u32[]{:S(2)}) copy-start(f32[32]{0:T(128)S(1)} %get-tuple-element.44) | copy-start | bytes 388
  90.3 49.0 %copy-start.18 = (f32[32]{0:T(128)}, f32[32]{0:T(128)S(1)}, u32[]{:S(2)}) copy-start(f32[32]{0:T(128)S(1)} %get-tuple-element.45) | copy-start | bytes 388
  90.3 49.0 %copy-start.20 = (f32[32]{0:T(128)}, f32[32]{0:T(128)S(1)}, u32[]{:S(2)}) copy-start(f32[32]{0:T(128)S(1)} %get-tuple-element.46) | copy-start | bytes 388
  90.3 49.0 %copy-start.22 = (f32[32]{0:T(128)}, f32[32]{0:T(128)S(1)}, u32[]{:S(2)}) copy-start(f32[32]{0:T(128)S(1)} %get-tuple-element.47) | copy-start | bytes 388
  90.3 49.0 %copy-start.24 = (f32[32]{0:T(128)}, f32[32]{0:T(128)S(1)}, u32[]{:S(2)}) copy-start(f32[32]{0:T(128)S(1)} %get-tuple-element.48) | copy-start | bytes 388
  90.3 49.0 %copy-start.26 = (f32[32]{0:T(128)}, f32[32]{0:T(128)S(1)}, u32[]{:S(2)}) copy-start(f32[32]{0:T(128)S(1)} %get-tuple-element.49) | copy-start | bytes 388
  90.3 49.0 %copy-start.28 = (f32[32]{0:T(128)}, f32[32]{0:T(128)S(1)}, u32[]{:S(2)}) copy-start(f32[32]{0:T(128)S(1)} %get-tuple-element.50) | copy-start | bytes 388
  90.3 48.9 %copy-start.30 = (f32[32]{0:T(128)}, f32[32]{0:T(128)S(1)}, u32[]{:S(2)}) copy-start(f32[32]{0:T(128)S(1)} %get-tuple-element.24) | copy-start | bytes 388
  90.3 48.9 %copy-start.32 = (f32[32]{0:T(128)}, f32[32]{0:T(128)S(1)}, u32[]{:S(2)}) copy-start(f32[32]{0:T(128)S(1)} %get-tuple-element.25) | copy-start | bytes 388
  90.4 48.9 %copy-start.34 = (f32[32]{0:T(128)}, f32[32]{0:T(128)S(1)}, u32[]{:S(2)}) copy-start(f32[32]{0:T(128)S(1)} %get-tuple-element.26) | copy-start | bytes 388
  90.4 48.9 %copy-start.36 = (f32[32]{0:T(128)}, f32[32]{0:T(128)S(1)}, u32[]{:S(2)}) copy-start(f32[32]{0:T(128)S(1)} %get-tuple-element.27) | copy-start | bytes 388
  90.4 48.9 %copy-start.38 = (f32[32]{0:T(128)}, f32[32]{0:T(128)S(1)}, u32[]{:S(2)}) copy-start(f32[32]{0:T(128)S(1)} %get-tuple-element.28) | copy-start | bytes 388
  90.4 48.9 %copy-start.40 = (f32[32]{0:T(128)}, f32[32]{0:T(128)S(1)}, u32[]{:S(2)}) copy-start(f32[32]{0:T(128)S(1)} %get-tuple-element.29) | copy-start | bytes 388
  90.4 48.9 %copy-start.42 = (f32[32]{0:T(128)}, f32[32]{0:T(128)S(1)}, u32[]{:S(2)}) copy-start(f32[32]{0:T(128)S(1)} %get-tuple-element.30) | copy-start | bytes 388
  90.4 48.9 %copy-start.44 = (f32[32]{0:T(128)}, f32[32]{0:T(128)S(1)}, u32[]{:S(2)}) copy-start(f32[32]{0:T(128)S(1)} %get-tuple-element.31) | copy-start | bytes 388
  90.4 48.9 %copy-start.46 = (f32[32]{0:T(128)}, f32[32]{0:T(128)S(1)}, u32[]{:S(2)}) copy-start(f32[32]{0:T(128)S(1)} %get-tuple-element.32) | copy-start | bytes 388
  90.4 48.9 %copy-start.48 = (f32[32]{0:T(128)}, f32[32]{0:T(128)S(1)}, u32[]{:S(2)}) copy-start(f32[32]{0:T(128)S(1)} %get-tuple-element.33) | copy-start | bytes 388
  90.4 48.9 %copy-start.50 = (f32[32]{0:T(128)}, f32[32]{0:T(128)S(1)}, u32[]{:S(2)}) copy-start(f32[32]{0:T(128)S(1)} %get-tuple-element.34) | copy-start | bytes 388
  90.4 48.9 %copy-start.52 = (f32[32]{0:T(128)}, f32[32]{0:T(128)S(1)}, u32[]{:S(2)}) copy-start(f32[32]{0:T(128)S(1)} %get-tuple-element.35) | copy-start | bytes 388
  90.5 48.9 %copy-start.54 = (f32[32]{0:T(128)}, f32[32]{0:T(128)S(1)}, u32[]{:S(2)}) copy-start(f32[32]{0:T(128)S(1)} %get-tuple-element.36) | copy-start | bytes 388
  90.5 48.9 %copy-start.56 = (f32[32]{0:T(128)}, f32[32]{0:T(128)S(1)}, u32[]{:S(2)}) copy-start(f32[32]{0:T(128)S(1)} %get-tuple-element.37) | copy-start | bytes 388
  90.5 48.9 %copy-start.58 = (f32[32]{0:T(128)}, f32[32]{0:T(128)S(1)}, u32[]{:S(2)}) copy-start(f32[32]{0:T(128)S(1)} %get-tuple-element.38) | copy-start | bytes 388
  90.5 48.9 %copy-start.60 = (f32[32]{0:T(128)}, f32[32]{0:T(128)S(1)}, u32[]{:S(2)}) copy-start(f32[32]{0:T(128)S(1)} %get-tuple-element.39) | copy-start | bytes 388
  90.5 48.9 %copy-start.62 = (f32[32]{0:T(128)}, f32[32]{0:T(128)S(1)}, u32[]{:S(2)}) copy-start(f32[32]{0:T(128)S(1)} %get-tuple-element.40) | copy-start | bytes 388
  90.5 48.9 %copy-start.64 = (f32[32]{0:T(128)}, f32[32]{0:T(128)S(1)}, u32[]{:S(2)}) copy-start(f32[32]{0:T(128)S(1)} %get-tuple-element.41) | copy-start | bytes 388
  90.5 48.9 %copy-start.66 = (f32[32]{0:T(128)}, f32[32]{0:T(128)S(1)}, u32[]{:S(2)}) copy-start(f32[32]{0:T(128)S(1)} %get-tuple-element.42) | copy-start | bytes 388
  112.6 224.4 %all-to-all-start.1 = ((f32[4,1,32768]{2,1,0:T(1,128)}), f32[4,1,32768]{2,1,0:T(1,128)S(1)}, u32[]{:S(2)}, u32[]{:S(2)}) async-start(f32[4,1,32768]{2,1,0:T(1,128)} %reshape.405), calls=%async_computation.1 | async-start | bytes 1048576 | tf_op jit(solution)/shard_map/all_to_all | solution.py:147
  349.8 36.1 %slice-start = ((s8[8388608]{0:T(1024)(128)(4,1)}), s8[4194304]{0:T(1024)(128)(4,1)S(1)}, s32[]{:S(2)}) async-start(s8[8388608]{0:T(1024)(128)(4,1)} %bitcast.460), calls=%async_computation.6 | async-start | bytes 8388608
  493.3 32.3 %all-to-all-start.2 = ((f32[4,1,32768]{2,1,0:T(1,128)}), f32[4,1,32768]{2,1,0:T(1,128)S(1)}, u32[]{:S(2)}, u32[]{:S(2)}) async-start(f32[4,1,32768]{2,1,0:T(1,128)} %reshape.407), calls=%async_computation.2 | async-start | bytes 1048576 | tf_op jit(solution)/shard_map/all_to_all | solution.py:141
  518.6 40.3 %collective-permute-start.3 = (bf16[1,32,1,128,128]{4,3,2,1,0:T(8,128)(2,1)}, bf16[1,32,1,128,128]{4,3,2,1,0:T(8,128)(2,1)}, u32[]{:S(2)}, u32[]{:S(2)}) collective-permute-start(bf16[1,32,1,128,128]{4,3,2,1,0:T(8,128)(2,1)} %get-tuple-element.19), channel_id=1, source_target_pairs={{1,0},{2,1},{3,2},{5,4},{6,5},{7,6},{9,8},{10,9},{11,10},{13,12},{... | collective-permute-start | bytes 3145736 | tf_op jit(solution)/shard_map/ppermute | solution.py:24
  519.9 39.0 %collective-permute-start.2 = (bf16[1,32,1,128,128]{4,3,2,1,0:T(8,128)(2,1)}, bf16[1,32,1,128,128]{4,3,2,1,0:T(8,128)(2,1)}, u32[]{:S(2)}, u32[]{:S(2)}) collective-permute-start(bf16[1,32,1,128,128]{4,3,2,1,0:T(8,128)(2,1)} %get-tuple-element.18), channel_id=1, source_target_pairs={{0,1},{1,2},{2,3},{4,5},{5,6},{6,7},{8,9},{9,10},{10,11},{12,13},{... | collective-permute-start | bytes 3145736 | tf_op jit(solution)/shard_map/ppermute | solution.py:23
  547.6 34.9 %all-to-all-start.3 = ((f32[4,1,32768]{2,1,0:T(1,128)}), f32[4,1,32768]{2,1,0:T(1,128)S(1)}, u32[]{:S(2)}, u32[]{:S(2)}) async-start(f32[4,1,32768]{2,1,0:T(1,128)} %reshape.409), calls=%async_computation.3 | async-start | bytes 1048576 | tf_op jit(solution)/shard_map/all_to_all | solution.py:147
  551.8 267.4 %reduce-scatter.2.cloned.1.call-start = ((), (), s32[]{:S(2)}) async-start(), calls=%async_computation.5 | async-start | bytes 10485760 | tf_op jit(solution)/shard_map/reduce_scatter | solution.py:185
  598.7 32.7 %copy-start.10 = (f32[8,128,128]{2,1,0:T(8,128)S(1)}, f32[8,128,128]{2,1,0:T(8,128)}, u32[]{:S(2)}) copy-start(f32[8,128,128]{2,1,0:T(8,128)} %multiply_bitcast_fusion) | copy-start | bytes 1572868
  598.7 32.7 %copy-start.15 = (f32[32]{0:T(128)S(1)}, f32[32]{0:T(128)}, u32[]{:S(2)}) copy-start(f32[32]{0:T(128)} %copy-done.14) | copy-start | bytes 388
  598.7 32.7 %copy-start.17 = (f32[32]{0:T(128)S(1)}, f32[32]{0:T(128)}, u32[]{:S(2)}) copy-start(f32[32]{0:T(128)} %copy-done.16) | copy-start | bytes 388
  598.7 32.7 %copy-start.19 = (f32[32]{0:T(128)S(1)}, f32[32]{0:T(128)}, u32[]{:S(2)}) copy-start(f32[32]{0:T(128)} %copy-done.18) | copy-start | bytes 388
  598.7 32.7 %copy-start.21 = (f32[32]{0:T(128)S(1)}, f32[32]{0:T(128)}, u32[]{:S(2)}) copy-start(f32[32]{0:T(128)} %copy-done.20) | copy-start | bytes 388
  598.7 32.7 %copy-start.23 = (f32[32]{0:T(128)S(1)}, f32[32]{0:T(128)}, u32[]{:S(2)}) copy-start(f32[32]{0:T(128)} %copy-done.22) | copy-start | bytes 388
  598.8 32.7 %copy-start.25 = (f32[32]{0:T(128)S(1)}, f32[32]{0:T(128)}, u32[]{:S(2)}) copy-start(f32[32]{0:T(128)} %copy-done.24) | copy-start | bytes 388
  598.8 32.7 %copy-start.27 = (f32[32]{0:T(128)S(1)}, f32[32]{0:T(128)}, u32[]{:S(2)}) copy-start(f32[32]{0:T(128)} %copy-done.26) | copy-start | bytes 388
  598.8 32.7 %copy-start.29 = (f32[32]{0:T(128)S(1)}, f32[32]{0:T(128)}, u32[]{:S(2)}) copy-start(f32[32]{0:T(128)} %copy-done.28) | copy-start | bytes 388
  598.8 32.7 %copy-start.31 = (f32[32]{0:T(128)S(1)}, f32[32]{0:T(128)}, u32[]{:S(2)}) copy-start(f32[32]{0:T(128)} %copy-done.30) | copy-start | bytes 388
  598.8 32.7 %copy-start.33 = (f32[32]{0:T(128)S(1)}, f32[32]{0:T(128)}, u32[]{:S(2)}) copy-start(f32[32]{0:T(128)} %copy-done.32) | copy-start | bytes 388
  598.8 32.7 %copy-start.35 = (f32[32]{0:T(128)S(1)}, f32[32]{0:T(128)}, u32[]{:S(2)}) copy-start(f32[32]{0:T(128)} %copy-done.34) | copy-start | bytes 388
  598.8 32.7 %copy-start.37 = (f32[32]{0:T(128)S(1)}, f32[32]{0:T(128)}, u32[]{:S(2)}) copy-start(f32[32]{0:T(128)} %copy-done.36) | copy-start | bytes 388
  598.8 32.7 %copy-start.39 = (f32[32]{0:T(128)S(1)}, f32[32]{0:T(128)}, u32[]{:S(2)}) copy-start(f32[32]{0:T(128)} %copy-done.38) | copy-start | bytes 388
  598.8 32.7 %copy-start.41 = (f32[32]{0:T(128)S(1)}, f32[32]{0:T(128)}, u32[]{:S(2)}) copy-start(f32[32]{0:T(128)} %copy-done.40) | copy-start | bytes 388
  598.8 32.7 %copy-start.43 = (f32[32]{0:T(128)S(1)}, f32[32]{0:T(128)}, u32[]{:S(2)}) copy-start(f32[32]{0:T(128)} %copy-done.42) | copy-start | bytes 388
  598.9 32.7 %copy-start.45 = (f32[32]{0:T(128)S(1)}, f32[32]{0:T(128)}, u32[]{:S(2)}) copy-start(f32[32]{0:T(128)} %copy-done.44) | copy-start | bytes 388
  598.9 32.7 %copy-start.47 = (f32[32]{0:T(128)S(1)}, f32[32]{0:T(128)}, u32[]{:S(2)}) copy-start(f32[32]{0:T(128)} %copy-done.46) | copy-start | bytes 388
  598.9 32.7 %copy-start.49 = (f32[32]{0:T(128)S(1)}, f32[32]{0:T(128)}, u32[]{:S(2)}) copy-start(f32[32]{0:T(128)} %copy-done.48) | copy-start | bytes 388
  598.9 32.7 %copy-start.51 = (f32[32]{0:T(128)S(1)}, f32[32]{0:T(128)}, u32[]{:S(2)}) copy-start(f32[32]{0:T(128)} %copy-done.50) | copy-start | bytes 388
  598.9 32.7 %copy-start.53 = (f32[32]{0:T(128)S(1)}, f32[32]{0:T(128)}, u32[]{:S(2)}) copy-start(f32[32]{0:T(128)} %copy-done.52) | copy-start | bytes 388
  598.9 32.7 %copy-start.55 = (f32[32]{0:T(128)S(1)}, f32[32]{0:T(128)}, u32[]{:S(2)}) copy-start(f32[32]{0:T(128)} %copy-done.54) | copy-start | bytes 388
  598.9 32.7 %copy-start.57 = (f32[32]{0:T(128)S(1)}, f32[32]{0:T(128)}, u32[]{:S(2)}) copy-start(f32[32]{0:T(128)} %copy-done.56) | copy-start | bytes 388
  598.9 32.7 %copy-start.59 = (f32[32]{0:T(128)S(1)}, f32[32]{0:T(128)}, u32[]{:S(2)}) copy-start(f32[32]{0:T(128)} %copy-done.58) | copy-start | bytes 388
  631.6 191.0 %copy-start.1 = (bf16[32,32]{1,0:T(8,128)(2,1)S(1)}, bf16[32,32]{1,0:T(8,128)(2,1)}, u32[]{:S(2)}) copy-start(bf16[32,32]{1,0:T(8,128)(2,1)} %param.11) | copy-start | bytes 6148
  (16 other events, 421.4 us)
Sparse Core Ops, SparseCore 0:
  559.0 73.1 reduce-scatter.1
where the time goes:
time: 833 us; the launch traced here: 830 us
  matrix products  452 us (54%)
  other arithmetic  279 us (33%)
  local copies, waits for them, and re-layouts  47.1 us (6%)
  starting transfers between devices  32.1 us (4%)
  between operations  15.8 us (2%)
    dot_general x2, matrix products, plane_inverse(): jnp.einsum('...xk,ky->...xy', imag_x, sin_y, precision=HIGHEST)  232 us
    another operation x1, other arithmetic  183 us
    dot_general x2, matrix products, plane_inverse(): jnp.einsum('...xk,ky->...xy', real_x, cos_y, precision=HIGHEST)  57.9 us
    concatenate x2, other arithmetic, extended(): shard = jnp.concatenate([before, shard, after], axis=dim)  46.6 us
    unnamed x156, local copies, waits for them, and re-layouts  26.3 us
    dot_general x2, matrix products, plane_forward(): jnp.einsum('...xk,jx->...jk', imag_y, sin_x, precision=HIGHEST)  17.1 us
    dot_general x2, matrix products, plane_forward(): jnp.einsum('...xk,jx->...jk', real_y, sin_x, precision=HIGHEST)  17.1 us
    dot_general x2, matrix products, plane_forward(): jnp.einsum('...xk,jx->...jk', imag_y, cos_x, precision=HIGHEST)  16.7 us
  transfers between devices with their start and end apart: 9, of which 1 were waited for; matrix products, arithmetic and copies ran while one was open for 74% of the time, Pallas kernels for 0%

commit v1 on v0

--- a/solution.py
+++ b/solution.py
@@ -138,7 +138,12 @@
         packed = packed.transpose(4, 5, 0, 3, 1, 2).reshape(
             KX * KY, samples_here, planes, 2 * channels
         )
-        moved = lax.all_to_all(packed, "slab", split_axis=0, concat_axis=2, tiled=True)
+        moved = jnp.concatenate(
+            lax.all_to_all(
+                jnp.stack(jnp.split(packed, lax.axis_size("slab"), axis=0)), "slab", 0, 0
+            ),
+            axis=2,
+        )
         summed = depth_forward(moved, cos_full, sin_full)
         return (summed[..., :channels], summed[..., channels:])
 

time: 833 us -> 853 us (1.024)
  local copies, waits for them, and re-layouts: 47.1 us -> 56.6 us
    split x0 -> x10, local copies, waits for them, and re-layouts: none -> 8.62 us  [to_modes(): jnp.split(packed, lax.axis_size('slab'), axis=0)]
    unnamed x3 -> x5, other arithmetic: 16.3 us -> 18.6 us
where the time goes in v1:
time: 853 us; the launch traced here: 850 us
  matrix products  459 us (54%)
  other arithmetic  283 us (33%)
  local copies, waits for them, and re-layouts  56.6 us (7%)
  starting transfers between devices  31.2 us (4%)
  between operations  15.9 us (2%)
    dot_general x2, matrix products, plane_inverse(): jnp.einsum('...xk,ky->...xy', imag_x, sin_y, precision=HIGHEST)  239 us
    another operation x1, other arithmetic  183 us
    dot_general x2, matrix products, plane_inverse(): jnp.einsum('...xk,ky->...xy', real_x, cos_y, precision=HIGHEST)  57.9 us
    concatenate x2, other arithmetic, extended(): shard = jnp.concatenate([before, shard, after], axis=dim)  46.5 us
    unnamed x156, local copies, waits for them, and re-layouts  26.9 us
    unnamed x5, other arithmetic  18.6 us
    dot_general x2, matrix products, plane_forward(): jnp.einsum('...xk,jx->...jk', imag_y, sin_x, precision=HIGHEST)  17.1 us
    dot_general x2, matrix products, plane_forward(): jnp.einsum('...xk,jx->...jk', real_y, sin_x, precision=HIGHEST)  17.1 us
  transfers between devices with their start and end apart: 9, of which 1 were waited for; matrix products, arithmetic and copies ran while one was open for 74% of the time, Pallas kernels for 0%

profile of v1, /device:TPU:0, one launch (start us, length us, event | category | flops | bytes accessed | tf_op | source)
XLA Modules:
  0.0 849.9 jit_solution(8695350587510628943)
XLA Ops:
  7.2 3.3 fusion.382
  10.5 1.4 collective-permute-start.1
  11.9 5.6 collective-permute-start
  17.5 9.4 %negate_bitcast_fusion = f32[32,8,128,16]{2,3,1,0:T(8,128)S(1)} fusion(bf16[1,32,8,128,128]{4,3,2,1,0:T(8,128)(2,1)} %param.7, s32[16]{0:T(128)S(1)} %compare_select_fusion.1), kind=kOutput, calls=%fused_computation.86 | convolution fusion | flops 805859328 | bytes 10485824 | tf_op jit(solution)/shard_map/...xy,ky->...xk/dot_general | solution.py:71
  26.9 6.8 fusion.67
  33.7 8.4 fusion.58
  42.1 8.6 %fusion.60 = f32[16,32,8,16]{1,0,3,2:T(8,128)S(1)} fusion(f32[32,8,128,16]{2,3,1,0:T(8,128)S(1)} %negate_bitcast_fusion, s32[16]{0:T(128)S(1)} %compare_select_fusion.1), kind=kOutput, calls=%fused_computation.97 | convolution fusion | flops 100691968 | bytes 2359360 | tf_op jit(solution)/shard_map/...xk,jx->...jk/dot_general | solution.py:72
  50.6 8.4 fusion.81
  59.0 8.4 fusion.75
  67.7 1.4 fusion.384
  69.8 1.4 copy.75
  72.3 1.4 copy.74
  74.8 1.8 copy.73
  77.6 2.2 fusion.386
  79.9 2.7 reshape.429
  82.6 4.3 all-to-all-start
  87.1 9.2 %copy.78 = bf16[64,16,2048]{0,2,1:T(8,128)(2,1)} copy(bf16[64,16,2048]{2,1,0:T(8,128)(2,1)} %param.9) | data formatting | bytes 8388608 | tf_op args[2]
  97.7 3.7 all-to-all-done
  102.0 3.9 reduce.16
  105.9 1.6 reshape.430
  108.5 2.2 copy.77
  112.9 6.4 fusion.23
  123.9 1.5 reshape.431
  125.3 3.5 all-to-all-start.1
  128.8 23.0 %select_maximum_fusion.2 = bf16[1,32,10,130,130]{4,3,2,1,0:T(8,128)(2,1)} fusion(bf16[1,32,1,128,128]{4,3,2,1,0:T(8,128)(2,1)S(1)} %collective-permute-done.1, bf16[1,32,8,128,128]{4,3,2,1,0:T(8,128)(2,1)} %param.7, bf16[1,32,1,128,128]{4,3,2,1,0:T(8,128)(2,1)S(1)} %collective-permute-done), kind=kLoop, calls=%fused_computation.9 | loop fusion | flops 102752000 | bytes 21301760 | tf_op jit(solution)/shard_map/concatenate | solution.py:25
  152.1 183.3 %fusion.39 = bf16[32,8,128,128]{3,2,1,0:T(8,128)(2,1)} fusion(bf16[1,32,10,130,130]{4,3,2,1,0:T(8,128)(2,1)} %select_maximum_fusion.2, f32[32]{0:T(128)S(1)} %get-tuple-element.57, f32[32]{0:T(128)S(1)} %get-tuple-element.58, f32[32]{0:T(128)S(1)} %get-tuple-element.33, f32[32]{0:T(128)S(1)} %get-tuple-element.34, ...), kind=kLoop, calls=%fused_computation.69 | loop fusion | flops 348127232 | bytes 220204416 | tf_op jit(solution)/shard_map/reshape.101
  335.5 14.3 %fusion.37 = f32[8,128,128,32]{2,3,1,0:T(8,128)} fusion(bf16[32,8,128,128]{3,2,1,0:T(8,128)(2,1)} %fusion.39, bf16[32,32]{1,0:T(8,128)(2,1)S(1)} %copy-done), kind=kOutput, calls=%fused_computation.65 | convolution fusion | flops 268435456 | bytes 25167872 | tf_op jit(solution)/shard_map/sczxy,co->sozxy/dot_general | solution.py:161
  349.7 2.2 reduce.17
  354.1 1.2 copy.253
  355.3 3.7 fusion.108
  359.0 3.5 fusion.109
  362.5 3.5 subtract_bitcast_fusion.2
  366.1 29.0 %fusion.48 = f32[32,8,128,128]{3,2,1,0:T(8,128)} fusion(f32[32,8,128,16]{2,0,3,1:T(8,128)S(1)} %subtract_bitcast_fusion.2, s32[16]{0:T(128)S(1)} %compare_select_fusion.1), kind=kOutput, calls=%fused_computation.79 | convolution fusion | flops 805335040 | bytes 18874432 | tf_op jit(solution)/shard_map/...xk,ky->...xy/dot_general | solution.py:88
  395.1 3.5 add_bitcast_fusion.2
  398.7 44.4 %fusion.40 = bf16[32,8,128,128]{3,2,1,0:T(8,128)(2,1)S(1)} fusion(f32[32]{0:T(128)S(1)} %copy-done.68, f32[8,128,128,32]{2,3,1,0:T(8,128)} %fusion.37, f32[8,128,128]{2,1,0:T(8,128)S(1)} %copy-done.9, f32[32,8,128,128]{3,2,1,0:T(8,128)} %fusion.48, bf16[1,32,8,128,128]{4,3,2,1,0:T(8,128)(2,1)S(1)} %bitcast.469, ...), kind=kOutput, calls=%fused_computation.70 | convolution fusion | flops 868249600 | bytes 52953280 | tf_op jit(solution)/shard_map/...xk,ky->...xy/dot_general | solution.py:88
  443.1 6.8 convolution_negate_fusion
  450.0 6.8 fusion.155
  456.8 8.4 fusion.50
  465.1 8.6 %fusion.52 = f32[16,32,8,16]{1,0,3,2:T(8,128)S(1)} fusion(f32[32,8,128,16]{2,3,1,0:T(8,128)S(1)} %convolution_negate_fusion, s32[16]{0:T(128)S(1)} %compare_select_fusion.1), kind=kOutput, calls=%fused_computation.89 | convolution fusion | flops 100691968 | bytes 2359360 | tf_op jit(solution)/shard_map/...xk,jx->...jk/dot_general | solution.py:72
  473.7 10.8 %fusion.35 = f32[8,128,128,32]{2,3,1,0:T(8,128)} fusion(bf16[32,8,128,128]{3,2,1,0:T(8,128)(2,1)S(1)} %fusion.40, bf16[32,32]{1,0:T(8,128)(2,1)S(1)} %copy-done), kind=kOutput, calls=%fused_computation.63 | convolution fusion | flops 268435456 | bytes 25167872 | tf_op jit(solution)/shard_map/sozxy,co->sczxy/dot_general | solution.py:202
  484.5 8.7 %fusion.93 = f32[1,1,32,8,16,16]{2,4,5,3,1,0:T(8,128)S(1)} fusion(f32[16,32,8,16]{1,0,3,2:T(8,128)S(1)} %fusion.50, f32[32,8,128,16]{2,3,1,0:T(8,128)S(1)} %fusion.155, s32[16]{0:T(128)S(1)} %compare_select_fusion.1), kind=kOutput, calls=%fused_computation.113 | convolution fusion | flops 100757504 | bytes 2621504 | tf_op jit(solution)/shard_map/...xk,jx->...jk/dot_general | solution.py:75
  493.3 8.4 fusion.87
  505.3 1.5 reshape.433
  506.8 5.2 all-to-all-start.2
  512.0 15.2 %fusion.66 = bf16[1,32,8,128,128]{4,3,2,1,0:T(8,128)(2,1)S(1)} fusion(f32[8,128,128,32]{2,3,1,0:T(8,128)} %fusion.35, f32[8,128,128]{2,1,0:T(8,128)S(1)} %copy-done.9), kind=kLoop, calls=%fused_computation.103 | loop fusion | flops 8388608 | bytes 25690112 | tf_op jit(solution)/shard_map/convert_element_type | solution.py:203
  527.2 3.3 copy-done.3
  530.6 1.4 fusion.381
  532.0 1.3 collective-permute-start.3
  533.3 5.7 collective-permute-start.2
  539.0 2.2 reduce.18
  545.0 10.0 %fusion.27 = (f32[64,16,32]{0,2,1:T(8,128)S(1)}, f32[64,16,32]{0,2,1:T(8,128)S(1)}, f32[64,16,32]{0,2,1:T(8,128)S(1)}, f32[64,16,32]{0,2,1:T(8,128)S(1)}) fusion(f32[64,16,32]{0,2,1:T(8,128)S(1)} %copy.160, bf16[64,16,2,32,32]{0,4,3,2,1:T(8,128)(2,1)} %bitcast.444, f32[64,16,32]{0,2,1:T(8,128)S(1)} %copy.161), kind=kLoop, calls=%fused_computation.51 | loop fusion | flops 10354688 | bytes 4980736
  559.6 1.5 reshape.435
  561.1 4.2 all-to-all-start.3
  565.3 2.5 add_bitcast_fusion
  567.8 4.6 fusion.4
  572.4 23.5 %select_maximum_fusion = bf16[1,32,10,130,130]{4,3,2,1,0:T(8,128)(2,1)} fusion(bf16[1,32,1,128,128]{4,3,2,1,0:T(8,128)(2,1)} %collective-permute-done.3, bf16[1,32,8,128,128]{4,3,2,1,0:T(8,128)(2,1)} %copy-done.3, bf16[1,32,1,128,128]{4,3,2,1,0:T(8,128)(2,1)} %collective-permute-done.2), kind=kLoop, calls=%fused_computation.7 | loop fusion | flops 102752000 | bytes 21301760 | tf_op jit(solution)/shard_map/concatenate | solution.py:25
  595.9 2.2 reduce.19
  601.5 3.5 fusion.110
  605.0 3.5 fusion.111
  608.5 3.7 subtract_bitcast_fusion.1
  612.5 28.8 %fusion.45 = f32[32,8,128,128]{3,2,1,0:T(8,128)} fusion(f32[32,8,128,16]{2,0,3,1:T(8,128)S(1)} %subtract_bitcast_fusion.1, s32[16]{0:T(128)S(1)} %compare_select_fusion.1), kind=kOutput, calls=%fused_computation.75 | convolution fusion | flops 805335040 | bytes 18874432 | tf_op jit(solution)/shard_map/...xk,ky->...xy/dot_general | solution.py:88
  641.3 3.5 add_bitcast_fusion.1
  645.2 194.1 %fusion.22 = bf16[1,32,8,128,128]{4,3,2,1,0:T(8,128)(2,1)} fusion(f32[32,8,128,128]{3,2,1,0:T(8,128)} %fusion.45, bf16[1,32,10,130,130]{4,3,2,1,0:T(8,128)(2,1)} %select_maximum_fusion, bf16[1,32,8,128,128]{4,3,2,1,0:T(8,128)(2,1)} %copy-done.3, bf16[1,32,1,128,128]{4,3,2,1,0:T(8,128)(2,1)} %collective-permute-done.2, ...), kind=kOutput, calls=%fused_computation.38 | convolution fusion | flops 1174433792 | bytes 256380352 | tf_op jit(solution)/shard_map/...xk,ky->...xy/dot_general | solution.py:88
  839.3 3.5 copy.108
  (212 shorter events, 31.3 us)
Async XLA Ops:
  7.2 328.3 %copy-start = (bf16[32,32]{1,0:T(8,128)(2,1)S(1)}, bf16[32,32]{1,0:T(8,128)(2,1)}, u32[]{:S(2)}) copy-start(bf16[32,32]{1,0:T(8,128)(2,1)} %param.11) | copy-start | bytes 6148
  10.5 118.4 %collective-permute-start.1 = (bf16[1,32,1,128,128]{4,3,2,1,0:T(8,128)(2,1)}, bf16[1,32,1,128,128]{4,3,2,1,0:T(8,128)(2,1)S(1)}, u32[]{:S(2)}, u32[]{:S(2)}) collective-permute-start(bf16[1,32,1,128,128]{4,3,2,1,0:T(8,128)(2,1)} %get-tuple-element.21), channel_id=1, source_target_pairs={{1,0},{2,1},{3,2},{5,4},{6,5},{7,6},{9,8},{10,9},{11,10},{13,12},{... | collective-permute-start | bytes 3145736 | tf_op jit(solution)/shard_map/ppermute | solution.py:24
  11.9 116.9 %collective-permute-start = (bf16[1,32,1,128,128]{4,3,2,1,0:T(8,128)(2,1)}, bf16[1,32,1,128,128]{4,3,2,1,0:T(8,128)(2,1)S(1)}, u32[]{:S(2)}, u32[]{:S(2)}) collective-permute-start(bf16[1,32,1,128,128]{4,3,2,1,0:T(8,128)(2,1)} %get-tuple-element.20), channel_id=1, source_target_pairs={{0,1},{1,2},{2,3},{4,5},{5,6},{6,7},{8,9},{9,10},{10,11},{12,13},{... | collective-permute-start | bytes 3145736 | tf_op jit(solution)/shard_map/ppermute | solution.py:23
  42.1 44.8 %copy-start.4 = (s32[1,8,128,128]{3,2,1,0:T(8,128)S(1)}, s32[1,8,128,128]{3,2,1,0:T(8,128)}, u32[]{:S(2)}) copy-start(s32[1,8,128,128]{3,2,1,0:T(8,128)} %param.8) | copy-start | bytes 1572868
  82.6 18.8 %all-to-all-start = ((f32[4,1,32768]{2,1,0:T(1,128)}), f32[4,1,32768]{2,1,0:T(1,128)}, u32[]{:S(2)}, u32[]{:S(2)}) async-start(f32[4,1,32768]{2,1,0:T(1,128)} %reshape.429), calls=%async_computation | async-start | bytes 1048576 | tf_op jit(solution)/shard_map/all_to_all | solution.py:142
  86.9 35.3 %copy-start.11 = (s32[16]{0:T(128)}, s32[16]{0:T(128)S(1)}, u32[]{:S(2)}) copy-start(s32[16]{0:T(128)S(1)} %compare_select_fusion) | copy-start | bytes 196
  97.4 54.5 %copy-start.14 = (f32[32]{0:T(128)}, f32[32]{0:T(128)S(1)}, u32[]{:S(2)}) copy-start(f32[32]{0:T(128)S(1)} %get-tuple-element.51) | copy-start | bytes 388
  97.4 54.5 %copy-start.16 = (f32[32]{0:T(128)}, f32[32]{0:T(128)S(1)}, u32[]{:S(2)}) copy-start(f32[32]{0:T(128)S(1)} %get-tuple-element.52) | copy-start | bytes 388
  97.4 54.5 %copy-start.18 = (f32[32]{0:T(128)}, f32[32]{0:T(128)S(1)}, u32[]{:S(2)}) copy-start(f32[32]{0:T(128)S(1)} %get-tuple-element.53) | copy-start | bytes 388
  97.4 54.5 %copy-start.20 = (f32[32]{0:T(128)}, f32[32]{0:T(128)S(1)}, u32[]{:S(2)}) copy-start(f32[32]{0:T(128)S(1)} %get-tuple-element.54) | copy-start | bytes 388
  97.4 54.5 %copy-start.22 = (f32[32]{0:T(128)}, f32[32]{0:T(128)S(1)}, u32[]{:S(2)}) copy-start(f32[32]{0:T(128)S(1)} %get-tuple-element.55) | copy-start | bytes 388
  97.4 54.5 %copy-start.24 = (f32[32]{0:T(128)}, f32[32]{0:T(128)S(1)}, u32[]{:S(2)}) copy-start(f32[32]{0:T(128)S(1)} %get-tuple-element.56) | copy-start | bytes 388
  97.4 54.5 %copy-start.26 = (f32[32]{0:T(128)}, f32[32]{0:T(128)S(1)}, u32[]{:S(2)}) copy-start(f32[32]{0:T(128)S(1)} %get-tuple-element.57) | copy-start | bytes 388
  97.5 54.5 %copy-start.28 = (f32[32]{0:T(128)}, f32[32]{0:T(128)S(1)}, u32[]{:S(2)}) copy-start(f32[32]{0:T(128)S(1)} %get-tuple-element.58) | copy-start | bytes 388
  97.5 54.4 %copy-start.30 = (f32[32]{0:T(128)}, f32[32]{0:T(128)S(1)}, u32[]{:S(2)}) copy-start(f32[32]{0:T(128)S(1)} %get-tuple-element.32) | copy-start | bytes 388
  97.5 54.4 %copy-start.32 = (f32[32]{0:T(128)}, f32[32]{0:T(128)S(1)}, u32[]{:S(2)}) copy-start(f32[32]{0:T(128)S(1)} %get-tuple-element.33) | copy-start | bytes 388
  97.5 54.4 %copy-start.34 = (f32[32]{0:T(128)}, f32[32]{0:T(128)S(1)}, u32[]{:S(2)}) copy-start(f32[32]{0:T(128)S(1)} %get-tuple-element.34) | copy-start | bytes 388
  97.5 54.4 %copy-start.36 = (f32[32]{0:T(128)}, f32[32]{0:T(128)S(1)}, u32[]{:S(2)}) copy-start(f32[32]{0:T(128)S(1)} %get-tuple-element.35) | copy-start | bytes 388
  97.5 54.4 %copy-start.38 = (f32[32]{0:T(128)}, f32[32]{0:T(128)S(1)}, u32[]{:S(2)}) copy-start(f32[32]{0:T(128)S(1)} %get-tuple-element.36) | copy-start | bytes 388
  97.5 54.4 %copy-start.40 = (f32[32]{0:T(128)}, f32[32]{0:T(128)S(1)}, u32[]{:S(2)}) copy-start(f32[32]{0:T(128)S(1)} %get-tuple-element.37) | copy-start | bytes 388
  97.5 54.4 %copy-start.42 = (f32[32]{0:T(128)}, f32[32]{0:T(128)S(1)}, u32[]{:S(2)}) copy-start(f32[32]{0:T(128)S(1)} %get-tuple-element.38) | copy-start | bytes 388
  97.6 54.4 %copy-start.44 = (f32[32]{0:T(128)}, f32[32]{0:T(128)S(1)}, u32[]{:S(2)}) copy-start(f32[32]{0:T(128)S(1)} %get-tuple-element.39) | copy-start | bytes 388
  97.6 54.4 %copy-start.46 = (f32[32]{0:T(128)}, f32[32]{0:T(128)S(1)}, u32[]{:S(2)}) copy-start(f32[32]{0:T(128)S(1)} %get-tuple-element.40) | copy-start | bytes 388
  97.6 54.4 %copy-start.48 = (f32[32]{0:T(128)}, f32[32]{0:T(128)S(1)}, u32[]{:S(2)}) copy-start(f32[32]{0:T(128)S(1)} %get-tuple-element.41) | copy-start | bytes 388
  97.6 54.4 %copy-start.50 = (f32[32]{0:T(128)}, f32[32]{0:T(128)S(1)}, u32[]{:S(2)}) copy-start(f32[32]{0:T(128)S(1)} %get-tuple-element.42) | copy-start | bytes 388
  97.6 54.4 %copy-start.52 = (f32[32]{0:T(128)}, f32[32]{0:T(128)S(1)}, u32[]{:S(2)}) copy-start(f32[32]{0:T(128)S(1)} %get-tuple-element.43) | copy-start | bytes 388
  97.6 54.4 %copy-start.54 = (f32[32]{0:T(128)}, f32[32]{0:T(128)S(1)}, u32[]{:S(2)}) copy-start(f32[32]{0:T(128)S(1)} %get-tuple-element.44) | copy-start | bytes 388
  97.6 54.4 %copy-start.56 = (f32[32]{0:T(128)}, f32[32]{0:T(128)S(1)}, u32[]{:S(2)}) copy-start(f32[32]{0:T(128)S(1)} %get-tuple-element.45) | copy-start | bytes 388
  97.6 54.4 %copy-start.58 = (f32[32]{0:T(128)}, f32[32]{0:T(128)S(1)}, u32[]{:S(2)}) copy-start(f32[32]{0:T(128)S(1)} %get-tuple-element.46) | copy-start | bytes 388
  97.6 54.4 %copy-start.60 = (f32[32]{0:T(128)}, f32[32]{0:T(128)S(1)}, u32[]{:S(2)}) copy-start(f32[32]{0:T(128)S(1)} %get-tuple-element.47) | copy-start | bytes 388
  97.6 54.4 %copy-start.62 = (f32[32]{0:T(128)}, f32[32]{0:T(128)S(1)}, u32[]{:S(2)}) copy-start(f32[32]{0:T(128)S(1)} %get-tuple-element.48) | copy-start | bytes 388
  97.7 54.4 %copy-start.64 = (f32[32]{0:T(128)}, f32[32]{0:T(128)S(1)}, u32[]{:S(2)}) copy-start(f32[32]{0:T(128)S(1)} %get-tuple-element.49) | copy-start | bytes 388
  97.7 54.4 %copy-start.66 = (f32[32]{0:T(128)}, f32[32]{0:T(128)S(1)}, u32[]{:S(2)}) copy-start(f32[32]{0:T(128)S(1)} %get-tuple-element.50) | copy-start | bytes 388
  125.3 224.4 %all-to-all-start.1 = ((f32[4,1,32768]{2,1,0:T(1,128)}), f32[4,1,32768]{2,1,0:T(1,128)S(1)}, u32[]{:S(2)}, u32[]{:S(2)}) async-start(f32[4,1,32768]{2,1,0:T(1,128)} %reshape.431), calls=%async_computation.1 | async-start | bytes 1048576 | tf_op jit(solution)/shard_map/all_to_all | solution.py:152
  362.5 36.1 %slice-start = ((s8[8388608]{0:T(1024)(128)(4,1)}), s8[4194304]{0:T(1024)(128)(4,1)S(1)}, s32[]{:S(2)}) async-start(s8[8388608]{0:T(1024)(128)(4,1)} %bitcast.468), calls=%async_computation.6 | async-start | bytes 8388608
  506.8 32.3 %all-to-all-start.2 = ((f32[4,1,32768]{2,1,0:T(1,128)}), f32[4,1,32768]{2,1,0:T(1,128)S(1)}, u32[]{:S(2)}, u32[]{:S(2)}) async-start(f32[4,1,32768]{2,1,0:T(1,128)} %reshape.433), calls=%async_computation.2 | async-start | bytes 1048576 | tf_op jit(solution)/shard_map/all_to_all | solution.py:142
  532.0 40.4 %collective-permute-start.3 = (bf16[1,32,1,128,128]{4,3,2,1,0:T(8,128)(2,1)}, bf16[1,32,1,128,128]{4,3,2,1,0:T(8,128)(2,1)}, u32[]{:S(2)}, u32[]{:S(2)}) collective-permute-start(bf16[1,32,1,128,128]{4,3,2,1,0:T(8,128)(2,1)} %get-tuple-element.19), channel_id=1, source_target_pairs={{1,0},{2,1},{3,2},{5,4},{6,5},{7,6},{9,8},{10,9},{11,10},{13,12},{... | collective-permute-start | bytes 3145736 | tf_op jit(solution)/shard_map/ppermute | solution.py:24
  533.3 39.1 %collective-permute-start.2 = (bf16[1,32,1,128,128]{4,3,2,1,0:T(8,128)(2,1)}, bf16[1,32,1,128,128]{4,3,2,1,0:T(8,128)(2,1)}, u32[]{:S(2)}, u32[]{:S(2)}) collective-permute-start(bf16[1,32,1,128,128]{4,3,2,1,0:T(8,128)(2,1)} %get-tuple-element.18), channel_id=1, source_target_pairs={{0,1},{1,2},{2,3},{4,5},{5,6},{6,7},{8,9},{9,10},{10,11},{12,13},{... | collective-permute-start | bytes 3145736 | tf_op jit(solution)/shard_map/ppermute | solution.py:23
  561.1 34.9 %all-to-all-start.3 = ((f32[4,1,32768]{2,1,0:T(1,128)}), f32[4,1,32768]{2,1,0:T(1,128)S(1)}, u32[]{:S(2)}, u32[]{:S(2)}) async-start(f32[4,1,32768]{2,1,0:T(1,128)} %reshape.435), calls=%async_computation.3 | async-start | bytes 1048576 | tf_op jit(solution)/shard_map/all_to_all | solution.py:152
  565.3 274.0 %reduce-scatter.2.cloned.1.call-start = ((), (), s32[]{:S(2)}) async-start(), calls=%async_computation.5 | async-start | bytes 10485760 | tf_op jit(solution)/shard_map/reduce_scatter | solution.py:190
  612.2 32.7 %copy-start.10 = (f32[8,128,128]{2,1,0:T(8,128)S(1)}, f32[8,128,128]{2,1,0:T(8,128)}, u32[]{:S(2)}) copy-start(f32[8,128,128]{2,1,0:T(8,128)} %multiply_bitcast_fusion) | copy-start | bytes 1572868
  612.2 32.7 %copy-start.15 = (f32[32]{0:T(128)S(1)}, f32[32]{0:T(128)}, u32[]{:S(2)}) copy-start(f32[32]{0:T(128)} %copy-done.14) | copy-start | bytes 388
  612.2 32.7 %copy-start.17 = (f32[32]{0:T(128)S(1)}, f32[32]{0:T(128)}, u32[]{:S(2)}) copy-start(f32[32]{0:T(128)} %copy-done.16) | copy-start | bytes 388
  612.2 32.7 %copy-start.19 = (f32[32]{0:T(128)S(1)}, f32[32]{0:T(128)}, u32[]{:S(2)}) copy-start(f32[32]{0:T(128)} %copy-done.18) | copy-start | bytes 388
  612.2 32.7 %copy-start.21 = (f32[32]{0:T(128)S(1)}, f32[32]{0:T(128)}, u32[]{:S(2)}) copy-start(f32[32]{0:T(128)} %copy-done.20) | copy-start | bytes 388
  612.3 32.7 %copy-start.23 = (f32[32]{0:T(128)S(1)}, f32[32]{0:T(128)}, u32[]{:S(2)}) copy-start(f32[32]{0:T(128)} %copy-done.22) | copy-start | bytes 388
  612.3 32.7 %copy-start.25 = (f32[32]{0:T(128)S(1)}, f32[32]{0:T(128)}, u32[]{:S(2)}) copy-start(f32[32]{0:T(128)} %copy-done.24) | copy-start | bytes 388
  612.3 32.7 %copy-start.27 = (f32[32]{0:T(128)S(1)}, f32[32]{0:T(128)}, u32[]{:S(2)}) copy-start(f32[32]{0:T(128)} %copy-done.26) | copy-start | bytes 388
  612.3 32.7 %copy-start.29 = (f32[32]{0:T(128)S(1)}, f32[32]{0:T(128)}, u32[]{:S(2)}) copy-start(f32[32]{0:T(128)} %copy-done.28) | copy-start | bytes 388
  612.3 32.7 %copy-start.31 = (f32[32]{0:T(128)S(1)}, f32[32]{0:T(128)}, u32[]{:S(2)}) copy-start(f32[32]{0:T(128)} %copy-done.30) | copy-start | bytes 388
  612.3 32.7 %copy-start.33 = (f32[32]{0:T(128)S(1)}, f32[32]{0:T(128)}, u32[]{:S(2)}) copy-start(f32[32]{0:T(128)} %copy-done.32) | copy-start | bytes 388
  612.3 32.7 %copy-start.35 = (f32[32]{0:T(128)S(1)}, f32[32]{0:T(128)}, u32[]{:S(2)}) copy-start(f32[32]{0:T(128)} %copy-done.34) | copy-start | bytes 388
  612.3 32.7 %copy-start.37 = (f32[32]{0:T(128)S(1)}, f32[32]{0:T(128)}, u32[]{:S(2)}) copy-start(f32[32]{0:T(128)} %copy-done.36) | copy-start | bytes 388
  612.3 32.7 %copy-start.39 = (f32[32]{0:T(128)S(1)}, f32[32]{0:T(128)}, u32[]{:S(2)}) copy-start(f32[32]{0:T(128)} %copy-done.38) | copy-start | bytes 388
  612.3 32.7 %copy-start.41 = (f32[32]{0:T(128)S(1)}, f32[32]{0:T(128)}, u32[]{:S(2)}) copy-start(f32[32]{0:T(128)} %copy-done.40) | copy-start | bytes 388
  612.4 32.7 %copy-start.43 = (f32[32]{0:T(128)S(1)}, f32[32]{0:T(128)}, u32[]{:S(2)}) copy-start(f32[32]{0:T(128)} %copy-done.42) | copy-start | bytes 388
  612.4 32.7 %copy-start.45 = (f32[32]{0:T(128)S(1)}, f32[32]{0:T(128)}, u32[]{:S(2)}) copy-start(f32[32]{0:T(128)} %copy-done.44) | copy-start | bytes 388
  612.4 32.7 %copy-start.47 = (f32[32]{0:T(128)S(1)}, f32[32]{0:T(128)}, u32[]{:S(2)}) copy-start(f32[32]{0:T(128)} %copy-done.46) | copy-start | bytes 388
  612.4 32.7 %copy-start.49 = (f32[32]{0:T(128)S(1)}, f32[32]{0:T(128)}, u32[]{:S(2)}) copy-start(f32[32]{0:T(128)} %copy-done.48) | copy-start | bytes 388
  612.4 32.7 %copy-start.51 = (f32[32]{0:T(128)S(1)}, f32[32]{0:T(128)}, u32[]{:S(2)}) copy-start(f32[32]{0:T(128)} %copy-done.50) | copy-start | bytes 388
  612.4 32.7 %copy-start.53 = (f32[32]{0:T(128)S(1)}, f32[32]{0:T(128)}, u32[]{:S(2)}) copy-start(f32[32]{0:T(128)} %copy-done.52) | copy-start | bytes 388
  612.4 32.7 %copy-start.55 = (f32[32]{0:T(128)S(1)}, f32[32]{0:T(128)}, u32[]{:S(2)}) copy-start(f32[32]{0:T(128)} %copy-done.54) | copy-start | bytes 388
  612.4 32.7 %copy-start.57 = (f32[32]{0:T(128)S(1)}, f32[32]{0:T(128)}, u32[]{:S(2)}) copy-start(f32[32]{0:T(128)} %copy-done.56) | copy-start | bytes 388
  645.1 197.7 %copy-start.1 = (bf16[32,32]{1,0:T(8,128)(2,1)S(1)}, bf16[32,32]{1,0:T(8,128)(2,1)}, u32[]{:S(2)}) copy-start(bf16[32,32]{1,0:T(8,128)(2,1)} %param.11) | copy-start | bytes 6148
  (16 other events, 431.4 us)
Sparse Core Ops, SparseCore 0:
  572.5 73.2 reduce-scatter.1
